TPU v7x, 512 devices: a whole 4x8x8 slice. The times are simulated.
512 devices in a mesh: seq: 32 (over x, y), head: 16 (over z, core).
Axes of the slice: x: 4, y: 8, z: 8, core: 2. Of those that a mesh axis runs over, the one named last changes fastest.
Arguments:
- queries: bfloat16 [65536, 2048], P(('seq', 'head')), may hold values from -6 to 6
- keys: bfloat16 [65536, 2048], P(('seq', 'head')), may hold values from -6 to 6
- values: bfloat16 [65536, 2048], P(('seq', 'head')), may hold values from -6 to 6
- log_decay: bfloat16 [65536, 16], P(('seq', 'head')), may hold values from -0.6 to 0, as said below
- out_weight: bfloat16 [2048, 2048], P(('seq', 'head')), may hold values from -0.125 to 0.125
Outputs:
- mixed_out: bfloat16 [65536, 2048], P(('seq', 'head'))
Inputs may be any that keep to these rules, and one draw needn't show every extreme that they name: `log_decay`: every entry is at most zero.
All inputs are finite; a program needn't handle non-finite values.
Results may differ from a plain program's by a relative error of at most 0.0054.
Values may be sent and summed in bfloat16 or wider, within the bound.
No kernel may reach another device: no remote copies, remote signals or barrier semaphores. Data moves between devices by JAX's collectives and lax.ppermute only.
A program may use at most 64 MiB of HBM per device.

v0:
```python
import jax
import jax.numpy as jnp
from jax import lax
from jax.sharding import PartitionSpec as P

SPAN = 256


def entering(x, axis, combine, identity):
    count, place = (lax.axis_size(axis), lax.axis_index(axis))
    everything = jax.tree.map(lambda part: lax.all_gather(part, axis), x)
    start = jax.tree.map(
        lambda part, zero: jnp.broadcast_to(jnp.asarray(zero, part.dtype), part.shape), x, identity
    )

    def turn(k, before):
        reached = k < place
        new = combine(before, jax.tree.map(lambda part: part[k], everything))
        return jax.tree.map(lambda a, b: jnp.where(reached, a, b), new, before)

    return lax.fori_loop(0, count, turn, start)


def local(queries, keys, values, log_decay, out_weight):
    queries_loc, keys_loc, values_loc, decay_loc = (
        lax.all_to_all(queries, "head", split_axis=1, concat_axis=0, tiled=True),
        lax.all_to_all(keys, "head", split_axis=1, concat_axis=0, tiled=True),
        lax.all_to_all(values, "head", split_axis=1, concat_axis=0, tiled=True),
        lax.all_to_all(log_decay, "head", split_axis=1, concat_axis=0, tiled=True),
    )
    shard_rows = queries_loc.shape[0]
    head_count = decay_loc.shape[1]
    head_dim = queries_loc.shape[1] // head_count
    block_count = shard_rows // SPAN
    queries_blk = queries_loc.reshape(block_count, SPAN, head_count, head_dim)
    keys_blk = keys_loc.reshape(block_count, SPAN, head_count, head_dim)
    values_blk = values_loc.reshape(block_count, SPAN, head_count, head_dim)
    within = jnp.cumsum(
        decay_loc.reshape(block_count, SPAN, head_count).astype(jnp.float32), axis=1
    )
    block_decay = within[:, -1, :]
    within_t = jnp.transpose(within, (0, 2, 1))
    causal = lax.broadcasted_iota(jnp.int32, (SPAN, SPAN), 0) >= lax.broadcasted_iota(
        jnp.int32, (SPAN, SPAN), 1
    )
    differences = within_t[:, :, :, None] - within_t[:, :, None, :]
    decay_mask = jnp.exp(jnp.where(causal[None, None], differences, -jnp.inf))
    scores = jnp.einsum(
        "nthd,nshd->nhts", queries_blk, keys_blk, preferred_element_type=jnp.float32
    )
    weights = (scores * decay_mask).astype(jnp.bfloat16)
    local_part = jnp.einsum(
        "nhts,nshd->nthd", weights, values_blk, preferred_element_type=jnp.float32
    )
    scaled_keys = (
        jnp.exp(block_decay[:, None, :] - within)[..., None] * keys_blk.astype(jnp.float32)
    ).astype(jnp.bfloat16)
    block_state = jnp.einsum(
        "nshd,nshe->nhde", scaled_keys, values_blk, preferred_element_type=jnp.float32
    )
    decay_incl = jnp.cumsum(block_decay, axis=0)
    decay_excl = decay_incl - block_decay
    block_index = lax.broadcasted_iota(jnp.int32, (block_count, block_count), 0)
    earlier_blocks = block_index > lax.broadcasted_iota(jnp.int32, (block_count, block_count), 1)
    pair_gaps = decay_excl[:, None, :] - decay_incl[None, :, :]
    block_weights = jnp.exp(jnp.where(earlier_blocks[:, :, None], pair_gaps, -jnp.inf))
    prior_states = jnp.einsum(
        "cjh,jhde->chde", block_weights, block_state, precision=lax.Precision.HIGHEST
    )
    total_decay = decay_incl[-1]
    final_state = jnp.einsum(
        "jh,jhde->hde",
        jnp.exp(total_decay[None, :] - decay_incl),
        block_state,
        precision=lax.Precision.HIGHEST,
    )

    def link(earlier, later):
        return (jnp.exp(later[1])[:, None, None] * earlier[0] + later[0], earlier[1] + later[1])

    incoming, _ = entering(
        (final_state, total_decay),
        "seq",
        link,
        (jnp.zeros_like(final_state), jnp.zeros_like(total_decay)),
    )
    full_states = prior_states + jnp.exp(decay_excl)[:, :, None, None] * incoming[None]
    scaled_queries = queries_blk.astype(jnp.float32) * jnp.exp(within)[..., None]
    carried_part = jnp.einsum(
        "nthd,nhde->nthe", scaled_queries, full_states, precision=lax.Precision.HIGHEST
    )
    combined = local_part + carried_part
    normed = (
        combined * lax.rsqrt(jnp.mean(combined * combined, axis=-1, keepdims=True) + 1e-05)
    ).astype(jnp.bfloat16)
    normed = normed.reshape(shard_rows, head_count * head_dim)
    restored = lax.all_to_all(normed, "head", split_axis=0, concat_axis=1, tiled=True)
    projected = jnp.dot(
        restored,
        lax.all_gather(out_weight, ("seq", "head"), axis=0, tiled=True),
        preferred_element_type=jnp.float32,
    )
    return projected.astype(jnp.bfloat16)


def solution(mesh):
    placed = (
        P(("seq", "head"), None),
        P(("seq", "head"), None),
        P(("seq", "head"), None),
        P(("seq", "head"), None),
        P(("seq", "head"), None),
    )
    return jax.shard_map(
        local, mesh=mesh, in_specs=placed, out_specs=P(("seq", "head"), None), check_vma=False
    )
```

profile of v0, /device:TPU:1, one launch (start us, length us, event | category | flops | bytes accessed | tf_op | source)
XLA Modules:
  0.0 307.7 jit_solution(8402958771548732288)
XLA Ops:
  6.5 1.3 copy.47
  7.9 11.8 %all-to-all-start.2 = ((bf16[128,16,1]{0,2,1:T(2,128)(2,1)}), bf16[128,16,1]{0,2,1:T(2,128)(2,1)S(1)}, u32[]{:S(2)}, u32[]{:S(2)}) async-start(bf16[128,16,1]{0,2,1:T(2,128)(2,1)} %copy.47), calls=%async_computation.2 | async-start | bytes 16384 | tf_op jit(solution)/shard_map/all_to_all | solution.py:29
  19.7 2.0 copy.45
  21.7 4.9 %all-to-all-done.2 = bf16[128,16,1]{0,2,1:T(2,128)(2,1)S(1)} async-done(((bf16[128,16,1]{0,2,1:T(2,128)(2,1)}), bf16[128,16,1]{0,2,1:T(2,128)(2,1)S(1)}, u32[]{:S(2)}, u32[]{:S(2)}) %all-to-all-start.2) | async-done | bytes 4128 | tf_op jit(solution)/shard_map/all_to_all | solution.py:29
  26.7 4.0 %all-to-all-start.1 = ((bf16[128,16,128]{0,2,1:T(8,128)(2,1)}), bf16[128,16,128]{0,2,1:T(8,128)(2,1)S(1)}, u32[]{:S(2)}, u32[]{:S(2)}) async-start(bf16[128,16,128]{0,2,1:T(8,128)(2,1)} %bitcast.2), calls=%async_computation.1 | async-start | bytes 1048576 | tf_op jit(solution)/shard_map/all_to_all | solution.py:27
  30.7 0.9 copy_bitcast_fusion
  32.4 15.6 %all-to-all-done.1 = bf16[128,16,128]{0,2,1:T(8,128)(2,1)S(1)} async-done(((bf16[128,16,128]{0,2,1:T(8,128)(2,1)}), bf16[128,16,128]{0,2,1:T(8,128)(2,1)S(1)}, u32[]{:S(2)}, u32[]{:S(2)}) %all-to-all-start.1) | async-done | bytes 524320 | tf_op jit(solution)/shard_map/all_to_all | solution.py:27
  48.0 3.5 %all-to-all-start.3 = ((bf16[128,16,128]{2,0,1:T(8,128)(2,1)}), bf16[128,16,128]{2,0,1:T(8,128)(2,1)S(1)}, u32[]{:S(2)}, u32[]{:S(2)}) async-start(bf16[128,16,128]{2,0,1:T(8,128)(2,1)} %copy_bitcast_fusion), calls=%async_computation.3 | async-start | bytes 1048576 | tf_op jit(solution)/shard_map/all_to_all | solution.py:28
  53.0 15.1 %all-to-all-done.3 = bf16[128,16,128]{2,0,1:T(8,128)(2,1)S(1)} async-done(((bf16[128,16,128]{2,0,1:T(8,128)(2,1)}), bf16[128,16,128]{2,0,1:T(8,128)(2,1)S(1)}, u32[]{:S(2)}, u32[]{:S(2)}) %all-to-all-start.3) | async-done | bytes 524320 | tf_op jit(solution)/shard_map/all_to_all | solution.py:28
  68.1 0.8 fusion.14
  68.9 2.0 fusion.18
  71.0 0.7 all-gather.7.cloned.1.call-update
  71.7 0.9 copy_bitcast_fusion.1
  72.6 3.5 %all-to-all-start = ((bf16[128,16,128]{2,0,1:T(8,128)(2,1)}), bf16[128,16,128]{2,0,1:T(8,128)(2,1)S(1)}, u32[]{:S(2)}, u32[]{:S(2)}) async-start(bf16[128,16,128]{2,0,1:T(8,128)(2,1)} %copy_bitcast_fusion.1), calls=%async_computation | async-start | bytes 1048576 | tf_op jit(solution)/shard_map/all_to_all | solution.py:26
  76.1 1.3 dynamic-slice
  77.5 1.1 bitcast_dynamic-update-slice_fusion
  78.7 61.9 %all-reduce = f32[32]{0:T(128)S(1)} all-reduce(f32[32]{0:T(128)S(1)} %bitcast_dynamic-update-slice_fusion), channel_id=1, replica_groups=mesh['seq'=32,'head'=16] {'seq'}, use_global_device_ids=true, to_apply=%add | all-reduce | flops 32 | bytes 256
  140.8 5.6 %all-gather.5.cloned.1.call-done = f32[4096,128]{1,0:T(8,128)} async-done(((f32[128,128]{1,0:T(8,128)}), f32[4096,128]{1,0:T(8,128)}) %all-gather.5.cloned.1.call-update) | async-done | bytes 2097168 | tf_op jit(solution)/shard_map/all_gather | solution.py:11
  146.4 64.9 %while.14 = (s32[]{:T(128)}, f32[1,128,128]{2,1,0:T(8,128)S(1)}, s32[]{:T(128)}, f32[32,1]{0,1:T(1,128)S(1)}, f32[32,1,128,128]{3,2,1,0:T(8,128)}, /*index=5*/s32[]{:T(128)}, s32[]{:T(128)}) while((s32[]{:T(128)}, f32[1,128,128]{2,1,0:T(8,128)S(1)}, s32[]{:T(128)}, f32[32,1]{0,1:T(1,128)S(1)}, f32[32,1,128,128]{3,2,1,0:T(8,128)}, ...), condition=%wide.region_4.5_spmd.clone, body=%wide.region_3.4_spmd.clone.sunk | while | flops 65540 | bytes 196733 | solution.py:21
  147.0 1.4 fusion.49
  149.0 1.4 fusion.49
  151.0 1.4 fusion.49
  152.5 0.6 fusion.48
  153.0 1.4 fusion.49
  155.1 1.4 fusion.49
  157.1 1.4 fusion.49
  159.1 1.4 fusion.49
  161.2 1.4 fusion.49
  163.2 1.4 fusion.49
  165.2 1.4 fusion.49
  167.3 1.4 fusion.49
  169.3 1.4 fusion.49
  171.3 1.4 fusion.49
  173.3 1.4 fusion.49
  175.4 1.4 fusion.49
  177.4 1.4 fusion.49
  179.4 1.4 fusion.49
  181.5 1.4 fusion.49
  183.5 1.4 fusion.49
  185.5 1.4 fusion.49
  187.6 1.4 fusion.49
  189.0 0.6 fusion.48
  189.6 1.4 fusion.49
  191.0 0.6 fusion.48
  191.6 1.4 fusion.49
  193.6 1.4 fusion.49
  195.7 1.4 fusion.49
  197.1 0.6 fusion.48
  197.7 1.4 fusion.49
  199.7 1.4 fusion.49
  201.8 1.4 fusion.49
  203.8 1.4 fusion.49
  205.8 1.4 fusion.49
  207.8 1.4 fusion.49
  209.9 1.4 fusion.49
  211.3 0.9 fusion.6
  212.2 2.2 fusion.7
  214.4 3.2 %multiply_reduce_fusion = (f32[8,256]{1,0:T(8,128)S(1)}, f32[8,1,128,256]{2,3,0,1:T(8,128)}) fusion(f32[8,128,256]{1,2,0:T(8,128)} %fusion.7, bf16[8,256,128]{2,1,0:T(8,128)(2,1)S(1)} %bitcast.101, bf16[8,256,128]{2,1,0:T(8,128)(2,1)S(1)} %bitcast.107, bf16[8,256,128]{2,1,0:T(8,128)(2,1)S(1)} %bitcast.103, f32[8,256]{1,0:T(8,128)S(1)} %get-tuple-element.129, ...), kind=kOutput, calls=%fused_computation.13 | convolution fusion | flops 271316992 | bytes 3751936 | tf_op jit(solution)/shard_map/nhts,nshd->nthd/dot_general | solution.py:52
  217.6 1.6 multiply_convert_fusion.1
  219.2 1.0 copy.55
  220.2 14.9 %all-to-all-start.4 = ((bf16[16,128,128]{1,2,0:T(8,128)(2,1)}), bf16[16,128,128]{1,2,0:T(8,128)(2,1)S(1)}, u32[]{:S(2)}, u32[]{:S(2)}) async-start(bf16[16,128,128]{1,2,0:T(8,128)(2,1)} %copy.55), calls=%async_computation.4 | async-start | bytes 1048576 | tf_op jit(solution)/shard_map/all_to_all | solution.py:97
  235.1 47.8 %all-gather.7.cloned.1.call-done = bf16[512,4,2048]{2,1,0:T(4,128)(2,1)} async-done(((bf16[1,4,2048]{2,1,0:T(4,128)(2,1)}), bf16[512,4,2048]{2,1,0:T(4,128)(2,1)}) %all-gather.7.cloned.1.call-update) | async-done | bytes 8388624 | tf_op jit(solution)/shard_map/all_gather | solution.py:100
  282.9 12.5 %reshape.334 = bf16[2048,2048]{1,0:T(8,128)(2,1)} reshape(bf16[512,4,2048]{2,1,0:T(4,128)(2,1)} %all-gather.7.cloned.1.call-done) | data formatting | bytes 16777216
  295.4 5.5 %convolution_convert_fusion = bf16[128,2048]{1,0:T(8,128)(2,1)} fusion(bf16[128,2048]{0,1:T(8,128)(2,1)S(1)} %bitcast.98, bf16[2048,2048]{1,0:T(8,128)(2,1)} %reshape.334), kind=kOutput, calls=%fused_computation.3 | convolution fusion | flops 1074003968 | bytes 9437184 | tf_op jit(solution)/shard_map/dot_general | solution.py:98
  (57 shorter events, 19.1 us)
Async XLA Ops:
  6.5 24.2 %copy-start = (bf16[128,2048]{1,0:T(8,128)(2,1)S(1)}, bf16[128,2048]{1,0:T(8,128)(2,1)}, u32[]{:S(2)}) copy-start(bf16[128,2048]{1,0:T(8,128)(2,1)} %param.9) | copy-start | bytes 1572868
  7.9 18.8 %all-to-all-start.2 = ((bf16[128,16,1]{0,2,1:T(2,128)(2,1)}), bf16[128,16,1]{0,2,1:T(2,128)(2,1)S(1)}, u32[]{:S(2)}, u32[]{:S(2)}) async-start(bf16[128,16,1]{0,2,1:T(2,128)(2,1)} %copy.47), calls=%async_computation.2 | async-start | bytes 16384 | tf_op jit(solution)/shard_map/all_to_all | solution.py:29
  26.7 21.3 %all-to-all-start.1 = ((bf16[128,16,128]{0,2,1:T(8,128)(2,1)}), bf16[128,16,128]{0,2,1:T(8,128)(2,1)S(1)}, u32[]{:S(2)}, u32[]{:S(2)}) async-start(bf16[128,16,128]{0,2,1:T(8,128)(2,1)} %bitcast.2), calls=%async_computation.1 | async-start | bytes 1048576 | tf_op jit(solution)/shard_map/all_to_all | solution.py:27
  32.4 39.3 %copy-start.1 = (bf16[128,2048]{1,0:T(8,128)(2,1)S(1)}, bf16[128,2048]{1,0:T(8,128)(2,1)}, u32[]{:S(2)}) copy-start(bf16[128,2048]{1,0:T(8,128)(2,1)} %param.7) | copy-start | bytes 1572868
  48.0 20.1 %all-to-all-start.3 = ((bf16[128,16,128]{2,0,1:T(8,128)(2,1)}), bf16[128,16,128]{2,0,1:T(8,128)(2,1)S(1)}, u32[]{:S(2)}, u32[]{:S(2)}) async-start(bf16[128,16,128]{2,0,1:T(8,128)(2,1)} %copy_bitcast_fusion), calls=%async_computation.3 | async-start | bytes 1048576 | tf_op jit(solution)/shard_map/all_to_all | solution.py:28
  51.5 94.9 %all-gather.5.cloned.1.call-start = ((), (), s32[]{:S(2)}) async-start(), calls=%async_computation.5 | async-start | bytes 2162688 | tf_op jit(solution)/shard_map/all_gather | solution.py:11
  70.9 211.9 %all-gather.7.cloned.1.call-start = ((), (), s32[]{:S(2)}) async-start(), calls=%async_computation.6 | async-start | bytes 8404992 | tf_op jit(solution)/shard_map/all_gather | solution.py:100
  72.6 139.6 %all-to-all-start = ((bf16[128,16,128]{2,0,1:T(8,128)(2,1)}), bf16[128,16,128]{2,0,1:T(8,128)(2,1)S(1)}, u32[]{:S(2)}, u32[]{:S(2)}) async-start(bf16[128,16,128]{2,0,1:T(8,128)(2,1)} %copy_bitcast_fusion.1), calls=%async_computation | async-start | bytes 1048576 | tf_op jit(solution)/shard_map/all_to_all | solution.py:26
  220.2 75.2 %all-to-all-start.4 = ((bf16[16,128,128]{1,2,0:T(8,128)(2,1)}), bf16[16,128,128]{1,2,0:T(8,128)(2,1)S(1)}, u32[]{:S(2)}, u32[]{:S(2)}) async-start(bf16[16,128,128]{1,2,0:T(8,128)(2,1)} %copy.55), calls=%async_computation.4 | async-start | bytes 1048576 | tf_op jit(solution)/shard_map/all_to_all | solution.py:97
Sparse Core Ops, SparseCore 0:
  71.1 75.2 all-gather.4
  150.9 131.8 all-gather.6
where the time goes:
time: 310 us; the launch traced here: 308 us
  waiting for transfers between devices  89.7 us (29%)
  blocking collectives  61.9 us (20%)
  other arithmetic  48.3 us (16%)
  local copies, waits for them, and re-layouts  41.1 us (13%)
  starting transfers between devices  37.7 us (12%)
  matrix products  14.5 us (5%)
  between operations  13.5 us (4%)
    unnamed x1, blocking collectives  61.9 us
    all_gather x1, waiting for transfers between devices, local(): lax.all_gather(out_weight, ('seq', 'head'), axis=0, tiled=True)  47.8 us
    select_n x32, other arithmetic, turn(): return jax.tree.map(lambda a, b: jnp.where(reached, a, b), new, before)  45.4 us
    exp x32, local copies, waits for them, and re-layouts, link(): jnp.exp(later[1])[:, None, None] * earlier[0] + later[0]  18.8 us
    unnamed x9, local copies, waits for them, and re-layouts  16.9 us
    all_to_all x1, waiting for transfers between devices, local(): lax.all_to_all(keys, 'head', split_axis=1, concat_axis=0, tiled=True)  15.6 us
    all_to_all x1, waiting for transfers between devices, local(): lax.all_to_all(values, 'head', split_axis=1, concat_axis=0, tiled=True)  15.1 us
    all_to_all x1, starting transfers between devices, local(): lax.all_to_all(normed, 'head', split_axis=0, concat_axis=1, tiled=True)  14.9 us
  transfers between devices with their start and end apart: 7, of which 5 were waited for; matrix products, arithmetic and copies ran while one was open for 31% of the time, Pallas kernels for 0%

commit v1 on v0

--- a/solution.py
+++ b/solution.py
@@ -97,7 +97,12 @@
     restored = lax.all_to_all(normed, "head", split_axis=0, concat_axis=1, tiled=True)
     projected = jnp.dot(
         restored,
-        lax.all_gather(out_weight, ("seq", "head"), axis=0, tiled=True),
+        jnp.concatenate(
+            lax.all_to_all(
+                jnp.stack([out_weight] * lax.axis_size(("seq", "head"))), ("seq", "head"), 0, 0
+            ),
+            axis=0,
+        ),
         preferred_element_type=jnp.float32,
     )
     return projected.astype(jnp.bfloat16)

time: 310 us -> 482 us (1.55)
  blocking collectives: 61.9 us -> 254 us
  waiting for transfers between devices: 89.7 us -> 43.6 us
  starting transfers between devices: 37.7 us -> 57.3 us
  local copies, waits for them, and re-layouts: 41.1 us -> 47 us
    unnamed x1, blocking collectives: 61.9 us -> 234 us
    all_gather x1 -> x0, waiting for transfers between devices: 47.8 us -> none  [local(): lax.all_gather(out_weight, ('seq', 'head'), axis=0, tiled=True)]
    all_to_all x0 -> x1, blocking collectives: none -> 20 us  [local(): lax.all_to_all(values, 'head', split_axis=1, concat_axis=0, tiled=True)]
    all_to_all x1, waiting for transfers between devices: 0.01 us -> 16.3 us  [local(): lax.all_to_all(queries, 'head', split_axis=1, concat_axis=0, tiled=True)]
    all_to_all x1, waiting for transfers between devices: 15.1 us -> 0.01 us  [local(): lax.all_to_all(jnp.stack([out_weight] * lax.axis_size(('seq', 'head'))),...]
    unnamed x9 -> x12, local copies, waits for them, and re-layouts: 16.9 us -> 3.48 us
    reshape x0 -> x1, local copies, waits for them, and re-layouts: none -> 12.5 us  [local(): jnp.concatenate(lax.all_to_all(jnp.stack([out_weight] * lax.axis_size(('s...]
    all_to_all x1, starting transfers between devices: 3.47 us -> 15.4 us  [local(): lax.all_to_all(jnp.stack([out_weight] * lax.axis_size(('seq', 'head'))),...]
  transfers between devices with their start and end apart: 7 -> 6, of which waited for: 5 -> 4; matrix products, arithmetic and copies ran while one was open for 31% -> 20% of each run, Pallas kernels for 0% -> 0%
where the time goes in v1:
time: 482 us; the launch traced here: 479 us
  blocking collectives  254 us (53%)
  starting transfers between devices  57.3 us (12%)
  other arithmetic  49.8 us (10%)
  local copies, waits for them, and re-layouts  47 us (10%)
  waiting for transfers between devices  43.6 us (9%)
  between operations  13.6 us (3%)
  matrix products  13.5 us (3%)
    unnamed x1, blocking collectives  234 us
    select_n x32, other arithmetic, turn(): return jax.tree.map(lambda a, b: jnp.where(reached, a, b), new, before)  48.1 us
    all_to_all x1, starting transfers between devices, local(): lax.all_to_all(normed, 'head', split_axis=0, concat_axis=1, tiled=True)  22.6 us
    all_to_all x1, blocking collectives, local(): lax.all_to_all(values, 'head', split_axis=1, concat_axis=0, tiled=True)  20 us
    exp x32, local copies, waits for them, and re-layouts, link(): jnp.exp(later[1])[:, None, None] * earlier[0] + later[0]  18.9 us
    all_to_all x1, waiting for transfers between devices, local(): lax.all_to_all(keys, 'head', split_axis=1, concat_axis=0, tiled=True)  16.5 us
    all_to_all x1, waiting for transfers between devices, local(): lax.all_to_all(queries, 'head', split_axis=1, concat_axis=0, tiled=True)  16.3 us
    all_to_all x1, starting transfers between devices, local(): lax.all_to_all(jnp.stack([out_weight] * lax.axis_size(('seq', 'head'))),...  15.4 us
  transfers between devices with their start and end apart: 6, of which 4 were waited for; matrix products, arithmetic and copies ran while one was open for 20% of the time, Pallas kernels for 0%

profile of v1, /device:TPU:1, one launch (start us, length us, event | category | flops | bytes accessed | tf_op | source)
XLA Modules:
  0.0 479.4 jit_solution(7149954915545224031)
XLA Ops:
  6.5 1.4 copy.47
  7.9 11.8 %all-to-all-start.2 = ((bf16[128,16,1]{0,2,1:T(2,128)(2,1)}), bf16[128,16,1]{0,2,1:T(2,128)(2,1)S(1)}, u32[]{:S(2)}, u32[]{:S(2)}) async-start(bf16[128,16,1]{0,2,1:T(2,128)(2,1)} %copy.47), calls=%async_computation.2 | async-start | bytes 16384 | tf_op jit(solution)/shard_map/all_to_all | solution.py:29
  19.8 0.9 copy_bitcast_fusion.1
  20.7 6.1 %all-to-all-done.2 = bf16[128,16,1]{0,2,1:T(2,128)(2,1)S(1)} async-done(((bf16[128,16,1]{0,2,1:T(2,128)(2,1)}), bf16[128,16,1]{0,2,1:T(2,128)(2,1)S(1)}, u32[]{:S(2)}, u32[]{:S(2)}) %all-to-all-start.2) | async-done | bytes 4128 | tf_op jit(solution)/shard_map/all_to_all | solution.py:29
  26.8 4.0 all-to-all-start
  30.8 1.0 copy.45
  31.8 16.3 %all-to-all-done = bf16[128,16,128]{2,0,1:T(8,128)(2,1)S(1)} async-done(((bf16[128,16,128]{2,0,1:T(8,128)(2,1)}), bf16[128,16,128]{2,0,1:T(8,128)(2,1)S(1)}, u32[]{:S(2)}, u32[]{:S(2)}) %all-to-all-start) | async-done | bytes 524320 | tf_op jit(solution)/shard_map/all_to_all | solution.py:26
  48.1 3.5 all-to-all-start.1
  51.7 16.5 %all-to-all-done.1 = bf16[128,16,128]{0,2,1:T(8,128)(2,1)S(1)} async-done(((bf16[128,16,128]{0,2,1:T(8,128)(2,1)}), bf16[128,16,128]{0,2,1:T(8,128)(2,1)S(1)}, u32[]{:S(2)}, u32[]{:S(2)}) %all-to-all-start.1) | async-done | bytes 524320 | tf_op jit(solution)/shard_map/all_to_all | solution.py:27
  68.2 20.0 %all_to_all.85 = bf16[128,16,128]{2,0,1:T(8,128)(2,1)S(1)} all-to-all(bf16[128,16,128]{2,0,1:T(8,128)(2,1)S(1)} %copy_bitcast_fusion), channel_id=1, replica_groups=mesh['seq'=32,'head'=16] {'head'}, dimensions={1} | all-to-all | bytes 1048576 | tf_op jit(solution)/shard_map/all_to_all | solution.py:28
  88.2 7.5 %stack.2 = bf16[512,4,2048]{2,1,0:T(4,128)(2,1)} broadcast(bf16[4,2048]{1,0:T(4,128)(2,1)S(1)} %copy-done.3), dimensions={1,2} | broadcast | bytes 8404992 | tf_op jit(solution)/shard_map/stack | solution.py:102
  95.7 15.4 %all-to-all-start.5 = ((bf16[512,4,2048]{2,1,0:T(4,128)(2,1)}), bf16[512,4,2048]{2,1,0:T(4,128)(2,1)}, u32[]{:S(2)}, u32[]{:S(2)}) async-start(bf16[512,4,2048]{2,1,0:T(4,128)(2,1)} %stack.2), calls=%async_computation.5 | async-start | bytes 16777216 | tf_op jit(solution)/shard_map/all_to_all | solution.py:101
  113.4 0.8 fusion.14
  114.2 2.0 fusion.18
  116.3 1.3 dynamic-slice
  117.7 1.2 bitcast_dynamic-update-slice_fusion
  118.8 233.8 %all-reduce = f32[32]{0:T(128)S(1)} all-reduce(f32[32]{0:T(128)S(1)} %bitcast_dynamic-update-slice_fusion), channel_id=1, replica_groups=mesh['seq'=32,'head'=16] {'seq'}, use_global_device_ids=true, to_apply=%add | all-reduce | flops 32 | bytes 256
  352.9 67.8 %while.14 = (s32[]{:T(128)}, f32[1,128,128]{2,1,0:T(8,128)S(1)}, s32[]{:T(128)}, f32[32,1]{0,1:T(1,128)S(1)}, f32[32,1,128,128]{3,2,1,0:T(8,128)}, /*index=5*/s32[]{:T(128)}, s32[]{:T(128)}) while((s32[]{:T(128)}, f32[1,128,128]{2,1,0:T(8,128)S(1)}, s32[]{:T(128)}, f32[32,1]{0,1:T(1,128)S(1)}, f32[32,1,128,128]{3,2,1,0:T(8,128)}, ...), condition=%wide.region_4.5_spmd.clone, body=%wide.region_3.4_spmd.clone.sunk | while | flops 65540 | bytes 196733 | solution.py:21
  353.5 1.5 fusion.49
  355.0 0.6 fusion.48
  355.6 1.5 fusion.49
  357.1 0.6 fusion.48
  357.7 1.5 fusion.49
  359.2 0.6 fusion.48
  359.8 1.5 fusion.49
  361.4 0.6 fusion.48
  361.9 1.5 fusion.49
  363.5 0.6 fusion.48
  364.1 1.5 fusion.49
  365.6 0.6 fusion.48
  366.2 1.5 fusion.49
  368.3 1.5 fusion.49
  370.4 1.5 fusion.49
  372.5 1.5 fusion.49
  374.7 1.5 fusion.49
  376.8 1.5 fusion.49
  378.9 1.5 fusion.49
  381.0 1.5 fusion.49
  383.1 1.5 fusion.49
  385.3 1.5 fusion.49
  387.4 1.5 fusion.49
  389.5 1.5 fusion.49
  391.6 1.5 fusion.49
  393.7 1.5 fusion.49
  395.8 1.5 fusion.49
  398.0 1.5 fusion.49
  400.1 1.5 fusion.49
  402.2 1.5 fusion.49
  404.3 1.5 fusion.49
  406.4 1.5 fusion.49
  408.6 1.5 fusion.49
  410.7 1.5 fusion.49
  412.8 1.5 fusion.49
  414.9 1.5 fusion.49
  417.0 1.5 fusion.49
  419.2 1.5 fusion.49
  420.7 0.9 fusion.6
  421.6 2.1 fusion.7
  423.7 2.2 multiply_reduce_fusion
  426.3 1.0 copy.55
  427.3 22.6 %all-to-all-start.4 = ((bf16[16,128,128]{1,2,0:T(8,128)(2,1)}), bf16[16,128,128]{1,2,0:T(8,128)(2,1)S(1)}, u32[]{:S(2)}, u32[]{:S(2)}) async-start(bf16[16,128,128]{1,2,0:T(8,128)(2,1)} %copy.55), calls=%async_computation.4 | async-start | bytes 1048576 | tf_op jit(solution)/shard_map/all_to_all | solution.py:97
  449.8 12.5 %reshape.333 = bf16[2048,2048]{1,0:T(8,128)(2,1)} reshape(bf16[512,4,2048]{2,1,0:T(4,128)(2,1)} %all-to-all-done.5) | data formatting | bytes 16777216 | tf_op jit(solution)/shard_map/reshape | solution.py:100
  462.3 4.7 all-to-all-done.4
  467.1 5.5 %convolution_convert_fusion = bf16[128,2048]{1,0:T(8,128)(2,1)} fusion(bf16[128,2048]{0,1:T(8,128)(2,1)S(1)} %bitcast.97, bf16[2048,2048]{1,0:T(8,128)(2,1)} %reshape.333), kind=kOutput, calls=%fused_computation.3 | convolution fusion | flops 1074003968 | bytes 9437184 | tf_op jit(solution)/shard_map/dot_general | solution.py:98
  (60 shorter events, 18.5 us)
Async XLA Ops:
  6.5 13.2 %copy-start = (bf16[128,2048]{1,0:T(8,128)(2,1)S(1)}, bf16[128,2048]{1,0:T(8,128)(2,1)}, u32[]{:S(2)}) copy-start(bf16[128,2048]{1,0:T(8,128)(2,1)} %param.7) | copy-start | bytes 1572868
  6.5 24.3 %copy-start.1 = (bf16[128,2048]{1,0:T(8,128)(2,1)S(1)}, bf16[128,2048]{1,0:T(8,128)(2,1)}, u32[]{:S(2)}) copy-start(bf16[128,2048]{1,0:T(8,128)(2,1)} %param.8) | copy-start | bytes 1572868
  7.9 18.9 %all-to-all-start.2 = ((bf16[128,16,1]{0,2,1:T(2,128)(2,1)}), bf16[128,16,1]{0,2,1:T(2,128)(2,1)S(1)}, u32[]{:S(2)}, u32[]{:S(2)}) async-start(bf16[128,16,1]{0,2,1:T(2,128)(2,1)} %copy.47), calls=%async_computation.2 | async-start | bytes 16384 | tf_op jit(solution)/shard_map/all_to_all | solution.py:29
  19.7 31.8 %copy-start.2 = (bf16[128,2048]{1,0:T(8,128)(2,1)S(1)}, bf16[128,2048]{1,0:T(8,128)(2,1)}, u32[]{:S(2)}) copy-start(bf16[128,2048]{1,0:T(8,128)(2,1)} %param.9) | copy-start | bytes 1572868
  26.8 21.3 %all-to-all-start = ((bf16[128,16,128]{2,0,1:T(8,128)(2,1)}), bf16[128,16,128]{2,0,1:T(8,128)(2,1)S(1)}, u32[]{:S(2)}, u32[]{:S(2)}) async-start(bf16[128,16,128]{2,0,1:T(8,128)(2,1)} %copy_bitcast_fusion.1), calls=%async_computation | async-start | bytes 1048576 | tf_op jit(solution)/shard_map/all_to_all | solution.py:26
  30.8 57.4 %copy-start.3 = (bf16[4,2048]{1,0:T(4,128)(2,1)S(1)}, bf16[4,2048]{1,0:T(4,128)(2,1)}, u32[]{:S(2)}) copy-start(bf16[4,2048]{1,0:T(4,128)(2,1)} %param.11) | copy-start | bytes 49156
  48.1 20.1 %all-to-all-start.1 = ((bf16[128,16,128]{0,2,1:T(8,128)(2,1)}), bf16[128,16,128]{0,2,1:T(8,128)(2,1)S(1)}, u32[]{:S(2)}, u32[]{:S(2)}) async-start(bf16[128,16,128]{0,2,1:T(8,128)(2,1)} %bitcast.2), calls=%async_computation.1 | async-start | bytes 1048576 | tf_op jit(solution)/shard_map/all_to_all | solution.py:27
  95.7 331.6 %all-to-all-start.5 = ((bf16[512,4,2048]{2,1,0:T(4,128)(2,1)}), bf16[512,4,2048]{2,1,0:T(4,128)(2,1)}, u32[]{:S(2)}, u32[]{:S(2)}) async-start(bf16[512,4,2048]{2,1,0:T(4,128)(2,1)} %stack.2), calls=%async_computation.5 | async-start | bytes 16777216 | tf_op jit(solution)/shard_map/all_to_all | solution.py:101
  111.1 241.8 %all-gather.3.cloned.1.call-start = ((), (), s32[]{:S(2)}) async-start(), calls=%async_computation.6 | async-start | bytes 2162688 | tf_op jit(solution)/shard_map/all_gather | solution.py:11
  427.3 39.8 %all-to-all-start.4 = ((bf16[16,128,128]{1,2,0:T(8,128)(2,1)}), bf16[16,128,128]{1,2,0:T(8,128)(2,1)S(1)}, u32[]{:S(2)}, u32[]{:S(2)}) async-start(bf16[16,128,128]{1,2,0:T(8,128)(2,1)} %copy.55), calls=%async_computation.4 | async-start | bytes 1048576 | tf_op jit(solution)/shard_map/all_to_all | solution.py:97
Sparse Core Ops, SparseCore 0:
  116.4 99.9 all-gather.2
